TPU v7x, 256 devices: a whole 4x4x8 slice. The times are simulated.
256 devices in a mesh: section: 32 (over x_hi, z, core), expert: 8 (over x_lo, y).
Axes of the slice: x: 4 (x_hi: 2, x_lo: 2; x = x_hi * 2 + x_lo), y: 4, z: 8, core: 2. Of those that a mesh axis runs over, the one named last changes fastest.
Arguments:
- tokens: bfloat16 [1536, 6144], P('expert', 'section'), may hold values from -6 to 6
- expert_ids: int32 [1536, 2], P('expert'), may hold values from 0 to 7, as said below
- slot_ids: int32 [1536, 2], P('expert'), may hold values from 0 to 47, as said below
- router: float32 [6144, 8], replicated, may hold values from -0.078125 to 0.078125
- up_weight: bfloat16 [8, 6144, 8192], P('expert', None, 'section'), may hold values from -0.078125 to 0.078125
- down_weight: bfloat16 [8, 8192, 6144], P('expert', 'section'), may hold values from -0.0625 to 0.0625
- cotangent: bfloat16 [1536, 6144], P('expert', 'section'), may hold values from -6 to 6
Outputs:
- mixed: bfloat16 [1536, 6144], P('expert', 'section')
- grad_tokens: bfloat16 [1536, 6144], P('expert', 'section')
- grad_up: bfloat16 [8, 6144, 8192], P('expert', None, 'section')
- grad_down: bfloat16 [8, 8192, 6144], P('expert', 'section')
- grad_router: float32 [6144, 8], replicated
Inputs may be any that keep to these rules, and one draw needn't show every extreme that they name: `expert_ids`: within each block of 192 consecutive tokens (one group), a token's two experts differ and every expert is chosen exactly 48 times. `slot_ids`: within each block of 192 consecutive tokens, the 48 choices of one expert take the slots 0 to 47 once each.
All inputs are finite; a program needn't handle non-finite values.
Results may differ from a plain program's by a relative error of at most 0.019.
Values may be sent and summed in bfloat16 or wider, within the bound.
A program may use at most 128 MiB of HBM per device.

v0:
```python
import jax
import jax.numpy as jnp
from jax import lax
from jax.sharding import PartitionSpec as P


def gate_values(logits, choose):
    picked = jnp.sum(logits[:, None, :] * choose, axis=2)
    logit_gap = picked[:, 0] - picked[:, 1]
    return jnp.stack([jax.nn.sigmoid(logit_gap), jax.nn.sigmoid(-logit_gap)], axis=1)


def dispatch_rows(slot_place, gate_pair, rows_in, rows_cot, slot_total):
    select = (
        jnp.arange(slot_total, dtype=jnp.int32)[:, None, None] == slot_place[None, :, :]
    ).astype(jnp.float32)
    gate_row = jnp.sum(select * gate_pair[None, :, :], axis=(1, 2))
    picker = jnp.sum(select, axis=2).astype(jnp.bfloat16)
    sent_in = jnp.dot(picker, rows_in, preferred_element_type=jnp.float32).astype(jnp.bfloat16)
    sent_cot = jnp.dot(picker, rows_cot, preferred_element_type=jnp.float32)
    sent_cot = (sent_cot * gate_row[:, None]).astype(jnp.bfloat16)
    return (sent_in, sent_cot)


def shards(tokens, expert_ids, slot_ids, router, up_weight, down_weight, cotangent):
    token_count, feat_slice = tokens.shape
    model_width, n_expert = router.shape
    slot_cap = 2 * token_count // n_expert
    slot_total = n_expert * slot_cap
    feat_start = lax.axis_index("section") * feat_slice
    router_rows = lax.dynamic_slice_in_dim(router, feat_start, feat_slice, 0)
    choose = (
        expert_ids[:, :, None] == jnp.arange(n_expert, dtype=jnp.int32)[None, None, :]
    ).astype(jnp.float32)
    slot_place = expert_ids * slot_cap + slot_ids
    full_in, full_cot = (
        lax.all_gather(tokens, "section", axis=1, tiled=True),
        lax.all_gather(cotangent, "section", axis=1, tiled=True),
    )
    logits = jnp.dot(full_in.astype(jnp.float32), router, precision=lax.Precision.HIGHEST)
    gate_pair = gate_values(logits, choose)
    sent_in, sent_cot = dispatch_rows(slot_place, gate_pair, full_in, full_cot, slot_total)
    block_shape = (n_expert, slot_cap, model_width)
    rows_in, rows_cot = (
        lax.all_to_all(
            sent_in.reshape(block_shape), "expert", split_axis=0, concat_axis=0, tiled=True
        ),
        lax.all_to_all(
            sent_cot.reshape(block_shape), "expert", split_axis=0, concat_axis=0, tiled=True
        ),
    )
    rows_in = rows_in.reshape(slot_total, model_width)
    rows_cot = rows_cot.reshape(slot_total, model_width)
    weight_in = up_weight[0]
    weight_out = down_weight[0]
    pre_act = jnp.dot(rows_in, weight_in, preferred_element_type=jnp.float32)
    sigma = jax.nn.sigmoid(pre_act)
    hidden = (pre_act * sigma).astype(jnp.bfloat16)
    hidden_grad = lax.dot_general(
        rows_cot, weight_out, (((1,), (1,)), ((), ())), preferred_element_type=jnp.float32
    )
    pre_grad = (hidden_grad * sigma * (1.0 + pre_act * (1.0 - sigma))).astype(jnp.bfloat16)
    grad_down = lax.dot_general(
        hidden, rows_cot, (((0,), (0,)), ((), ())), preferred_element_type=jnp.float32
    ).astype(jnp.bfloat16)
    grad_up = lax.dot_general(
        rows_in, pre_grad, (((0,), (0,)), ((), ())), preferred_element_type=jnp.float32
    ).astype(jnp.bfloat16)
    forward_part = jnp.dot(hidden, weight_out, preferred_element_type=jnp.float32)
    backward_part = lax.dot_general(
        pre_grad, weight_in, (((1,), (1,)), ((), ())), preferred_element_type=jnp.float32
    )
    out_sum, back_sum = (
        lax.psum_scatter(
            forward_part.astype(jnp.bfloat16), "section", scatter_dimension=1, tiled=True
        ).astype(jnp.float32),
        lax.psum_scatter(
            backward_part.astype(jnp.bfloat16), "section", scatter_dimension=1, tiled=True
        ).astype(jnp.float32),
    )
    return_shape = (n_expert, slot_cap, feat_slice)
    came_out, came_back = (
        lax.all_to_all(
            out_sum.astype(jnp.bfloat16).reshape(return_shape),
            "expert",
            split_axis=0,
            concat_axis=0,
            tiled=True,
        ),
        lax.all_to_all(
            back_sum.astype(jnp.bfloat16).reshape(return_shape),
            "expert",
            split_axis=0,
            concat_axis=0,
            tiled=True,
        ),
    )
    flat_out = came_out.reshape(slot_total, feat_slice)
    flat_back = came_back.reshape(slot_total, feat_slice)
    positions = jnp.arange(slot_total, dtype=jnp.int32)
    take_first = (slot_place[:, 0:1] == positions[None, :]).astype(jnp.bfloat16)
    take_second = (slot_place[:, 1:2] == positions[None, :]).astype(jnp.bfloat16)
    out_first = jnp.dot(take_first, flat_out, preferred_element_type=jnp.float32)
    out_second = jnp.dot(take_second, flat_out, preferred_element_type=jnp.float32)
    mixed = gate_pair[:, 0:1] * out_first + gate_pair[:, 1:2] * out_second
    cot_float = cotangent.astype(jnp.float32)
    grad_first, grad_second = lax.psum(
        (jnp.sum(cot_float * out_first, axis=1), jnp.sum(cot_float * out_second, axis=1)), "section"
    )
    logit_grad = (grad_first - grad_second) * gate_pair[:, 0] * gate_pair[:, 1]
    logits_grad = (choose[:, 0, :] - choose[:, 1, :]) * logit_grad[:, None]
    back_first = jnp.dot(take_first, flat_back, preferred_element_type=jnp.float32)
    back_second = jnp.dot(take_second, flat_back, preferred_element_type=jnp.float32)
    grad_tokens = (
        back_first
        + back_second
        + jnp.dot(logits_grad, router_rows.T, precision=lax.Precision.HIGHEST)
    )
    local_router = jnp.dot(
        tokens.astype(jnp.float32).T, logits_grad, precision=lax.Precision.HIGHEST
    )
    placed_router = lax.dynamic_update_slice(
        jnp.zeros((model_width, n_expert), jnp.float32), local_router, (feat_start, jnp.int32(0))
    )
    grad_router = lax.psum(placed_router, ("section", "expert"))
    return (
        mixed.astype(jnp.bfloat16),
        grad_tokens.astype(jnp.bfloat16),
        grad_up[None],
        grad_down[None],
        grad_router,
    )


def solution(mesh):
    in_specs = (
        P("expert", "section"),
        P("expert", None),
        P("expert", None),
        P(),
        P("expert", None, "section"),
        P("expert", "section", None),
        P("expert", "section"),
    )
    out_specs = (
        P("expert", "section"),
        P("expert", "section"),
        P("expert", None, "section"),
        P("expert", "section", None),
        P(),
    )
    return jax.shard_map(shards, mesh=mesh, in_specs=in_specs, out_specs=out_specs, check_vma=False)
```

profile of v0, /device:TPU:1, one launch (start us, length us, event | category | flops | bytes accessed | tf_op | source)
XLA Modules:
  0.0 798.1 jit_solution(7832499318834523150)
XLA Ops:
  7.2 1.8 copy.35
  9.7 88.7 %all-gather.3.cloned.1.call-done = bf16[192,6144]{0,1:T(8,128)(2,1)} async-done(((bf16[192,192]{0,1:T(8,128)(2,1)}), bf16[192,6144]{0,1:T(8,128)(2,1)}) %all-gather.3.cloned.1.call-update) | async-done | bytes 2359312 | tf_op jit(solution)/shard_map/all_gather | solution.py:37
  98.5 3.4 fusion.39
  103.4 3.7 convolution_convert_fusion.2
  107.0 4.7 all-to-all-start
  112.6 53.5 %all-to-all-done = bf16[8,48,6144]{2,1,0:T(8,128)(2,1)} async-done(((bf16[8,48,6144]{2,1,0:T(8,128)(2,1)}), bf16[8,48,6144]{2,1,0:T(8,128)(2,1)}, u32[]{:S(2)}, u32[]{:S(2)}) %all-to-all-start) | async-done | bytes 4718624 | tf_op jit(solution)/shard_map/all_to_all | solution.py:45
  166.2 4.7 fusion.6
  170.9 4.1 convolution_convert_fusion.1
  175.1 21.7 %all-gather.5.cloned.1.call-done = bf16[192,6144]{0,1:T(8,128)(2,1)} async-done(((bf16[192,192]{0,1:T(8,128)(2,1)}), bf16[192,6144]{0,1:T(8,128)(2,1)}) %all-gather.5.cloned.1.call-update) | async-done | bytes 2359312 | tf_op jit(solution)/shard_map/all_gather | solution.py:38
  196.7 3.8 multiply_convert_fusion
  200.6 61.3 %all_to_all.20 = bf16[8,48,6144]{2,1,0:T(8,128)(2,1)S(1)} all-to-all(bf16[8,48,6144]{2,1,0:T(8,128)(2,1)S(1)} %bitcast.60), channel_id=1, replica_groups=mesh['section'=32,'expert'=8] {'expert'}, dimensions={0} | all-to-all | bytes 9437184 | tf_op jit(solution)/shard_map/all_to_all | solution.py:48
  261.9 2.1 copy-done.1
  264.0 1.4 fusion.14
  266.1 4.0 convolution_convert_fusion
  271.4 5.9 fusion
  277.3 49.2 %reduce-scatter.3.cloned.1.call-done = bf16[384,192]{0,1:T(8,128)(2,1)} async-done(((bf16[384,6144]{0,1:T(8,128)(2,1)}), bf16[384,192]{0,1:T(8,128)(2,1)}) %reduce-scatter.3.cloned.1.call-update) | async-done | bytes 147472 | tf_op jit(solution)/shard_map/reduce_scatter | solution.py:74
  326.5 1.7 copy.36
  328.2 4.9 all-to-all-start.1
  333.1 5.9 fusion.1
  338.9 121.7 %reduce-scatter.5.cloned.1.call-done = bf16[384,192]{0,1:T(8,128)(2,1)} async-done(((bf16[384,6144]{0,1:T(8,128)(2,1)}), bf16[384,192]{0,1:T(8,128)(2,1)}) %reduce-scatter.5.cloned.1.call-update) | async-done | bytes 147472 | tf_op jit(solution)/shard_map/reduce_scatter | solution.py:77
  460.6 1.7 copy.38
  462.3 3.8 all-to-all-start.3
  466.2 1.2 fusion.21
  467.4 2.0 fusion.23
  469.4 70.1 %all-reduce = (f32[192]{0:T(256)S(1)}, f32[192]{0:T(256)S(1)}) all-reduce(f32[192]{0:T(256)S(1)} %get-tuple-element.26, f32[192]{0:T(256)S(1)} %get-tuple-element.25), channel_id=1, replica_groups=mesh['section'=32,'expert'=8] {'section'}, use_global_device_ids=true, to_apply=%region_6.0 | all-reduce | flops 384 | bytes 3072 | tf_op jit(solution)/shard_map/psum | solution.py:107
  540.7 1.7 convolution_bitcast_fusion
  544.0 1.1 fusion.33
  545.1 0.9 fusion.20
  546.0 1.6 fusion.18
  547.6 1.6 copy.40
  549.2 240.7 %all-reduce.3.cloned.1.call-done = f32[6144,8]{0,1:T(8,128)} async-done(((f32[6144,8]{0,1:T(8,128)}), f32[6144,8]{0,1:T(8,128)}) %all-reduce.3.cloned.1.call-update) | async-done | bytes 196624 | tf_op jit(solution)/shard_map/psum | solution.py:125
  789.9 1.6 copy.43
  (45 shorter events, 8.0 us)
Async XLA Ops:
  7.2 163.7 %copy-start = (bf16[1,256,6144]{2,1,0:T(8,128)(2,1)S(1)}, bf16[1,256,6144]{2,1,0:T(8,128)(2,1)}, u32[]{:S(2)}) copy-start(bf16[1,256,6144]{2,1,0:T(8,128)(2,1)} %param.12) | copy-start | bytes 9437188
  7.2 91.3 %all-gather.3.cloned.1.call-start = ((), (), s32[]{:S(2)}) async-start(), calls=%async_computation.6 | async-start | bytes 3244032 | tf_op jit(solution)/shard_map/all_gather | solution.py:37
  98.5 4.9 copy-start.2
  102.6 0.6 copy-start.10
  102.6 0.6 copy-start.9
  103.3 3.7 copy-start.4
  107.0 4.8 copy-start.7
  107.0 59.1 %all-to-all-start = ((bf16[8,48,6144]{2,1,0:T(8,128)(2,1)}), bf16[8,48,6144]{2,1,0:T(8,128)(2,1)}, u32[]{:S(2)}, u32[]{:S(2)}) async-start(bf16[8,48,6144]{2,1,0:T(8,128)(2,1)} %bitcast.59), calls=%async_computation | async-start | bytes 9437184 | tf_op jit(solution)/shard_map/all_to_all | solution.py:45
  111.8 85.0 %all-gather.5.cloned.1.call-start = ((), (), s32[]{:S(2)}) async-start(), calls=%async_computation.8 | async-start | bytes 3244032 | tf_op jit(solution)/shard_map/all_gather | solution.py:38
  112.6 213.9 %reduce-scatter.3.cloned.1.call-start = ((), (), s32[]{:S(2)}) async-start(), calls=%async_computation.7 | async-start | bytes 4866048 | tf_op jit(solution)/shard_map/reduce_scatter | solution.py:74
  175.0 285.6 %reduce-scatter.5.cloned.1.call-start = ((), (), s32[]{:S(2)}) async-start(), calls=%async_computation.9 | async-start | bytes 4866048 | tf_op jit(solution)/shard_map/reduce_scatter | solution.py:77
  261.9 2.1 copy-start.1
  264.0 2.1 copy-start.3
  265.4 0.7 copy-start.6
  328.2 134.1 %all-to-all-start.1 = ((bf16[8,48,192]{2,1,0:T(8,128)(2,1)}), bf16[8,48,192]{2,1,0:T(8,128)(2,1)}, u32[]{:S(2)}, u32[]{:S(2)}) async-start(bf16[8,48,192]{2,1,0:T(8,128)(2,1)} %bitcast.63), calls=%async_computation.2 | async-start | bytes 393216 | tf_op jit(solution)/shard_map/all_to_all | solution.py:83
  462.3 82.7 %all-to-all-start.3 = ((bf16[8,48,192]{2,1,0:T(8,128)(2,1)}), bf16[8,48,192]{2,1,0:T(8,128)(2,1)S(1)}, u32[]{:S(2)}, u32[]{:S(2)}) async-start(bf16[8,48,192]{2,1,0:T(8,128)(2,1)} %bitcast.12), calls=%async_computation.5 | async-start | bytes 393216 | tf_op jit(solution)/shard_map/all_to_all | solution.py:90
  466.1 323.8 %all-reduce.3.cloned.1.call-start = ((), (), s32[]{:S(2)}) async-start(), calls=%async_computation.10 | async-start | bytes 393216 | tf_op jit(solution)/shard_map/psum | solution.py:125
  540.1 0.6 copy-start.8
  543.3 0.7 copy-start.5
Sparse Core Ops, SparseCore 0:
  11.3 87.0 all-gather.2
  115.9 80.7 all-gather.4
  201.0 125.4 reduce-scatter.2
  330.6 129.9 reduce-scatter.4
  544.1 245.8 all-reduce.2
where the time goes:
time: 799 us; the launch traced here: 798 us
  waiting for transfers between devices  576 us (72%)
  blocking collectives  131 us (16%)
  matrix products  45.3 us (6%)
  local copies, waits for them, and re-layouts  15.4 us (2%)
  between operations  14 us (2%)
  starting transfers between devices  13.5 us (2%)
    psum x1, waiting for transfers between devices, shards(): grad_router = lax.psum(placed_router, ('section', 'expert'))  241 us
    reduce_scatter x1, waiting for transfers between devices, shards(): lax.psum_scatter(backward_part.astype(jnp.bfloat16), 'section', scatter_d...  122 us
    all_gather x1, waiting for transfers between devices, shards(): lax.all_gather(tokens, 'section', axis=1, tiled=True)  88.7 us
    psum x1, blocking collectives, shards(): lax.psum((jnp.sum(cot_float * out_first, axis=1), jnp.sum(cot_float * out...  70.1 us
    all_to_all x1, blocking collectives, shards(): lax.all_to_all(sent_cot.reshape(block_shape), 'expert', split_axis=0, con...  61.3 us
    all_to_all x1, waiting for transfers between devices, shards(): lax.all_to_all(sent_in.reshape(block_shape), 'expert', split_axis=0, conc...  53.5 us
    reduce_scatter x1, waiting for transfers between devices, shards(): lax.psum_scatter(forward_part.astype(jnp.bfloat16), 'section', scatter_di...  49.2 us
    all_gather x1, waiting for transfers between devices, shards(): lax.all_gather(cotangent, 'section', axis=1, tiled=True)  21.7 us
  transfers between devices with their start and end apart: 8, of which 6 were waited for; matrix products, arithmetic and copies ran while one was open for 6% of the time, Pallas kernels for 0%

commit v1 on v0

--- a/solution.py
+++ b/solution.py
@@ -23,6 +23,12 @@
 
 
 def shards(tokens, expert_ids, slot_ids, router, up_weight, down_weight, cotangent):
+
+    def run_panel(local):
+        work_now = lax.all_gather(local, axis_name=("section", "expert"))
+        tall = jnp.sum(work_now, axis=0)
+        return tall
+
     token_count, feat_slice = tokens.shape
     model_width, n_expert = router.shape
     slot_cap = 2 * token_count // n_expert
@@ -122,7 +128,7 @@
     placed_router = lax.dynamic_update_slice(
         jnp.zeros((model_width, n_expert), jnp.float32), local_router, (feat_start, jnp.int32(0))
     )
-    grad_router = lax.psum(placed_router, ("section", "expert"))
+    grad_router = run_panel(placed_router)
     return (
         mixed.astype(jnp.bfloat16),
         grad_tokens.astype(jnp.bfloat16),

time: 799 us -> 1270 us (1.59)
  waiting for transfers between devices: 576 us -> 1030 us
  other arithmetic: 2.99 us -> 20 us
    all_gather x0 -> x1, waiting for transfers between devices: none -> 763 us  [run_panel(): work_now = lax.all_gather(local, axis_name=('section', 'expert'))]
    psum x1 -> x0, waiting for transfers between devices: 241 us -> none  [shards(): grad_router = lax.psum(placed_router, ('section', 'expert'))]
    reduce_scatter x1, waiting for transfers between devices: 122 us -> 35.8 us  [shards(): lax.psum_scatter(backward_part.astype(jnp.bfloat16), 'section', scatter_d...]
    reduce_sum x0 -> x1, other arithmetic: none -> 18.4 us  [run_panel(): tall = jnp.sum(work_now, axis=0)]
  transfers between devices with their start and end apart: 8 -> 8, of which waited for: 6 -> 8; matrix products, arithmetic and copies ran while one was open for 6% -> 3% of each run, Pallas kernels for 0% -> 0%
where the time goes in v1:
time: 1270 us; the launch traced here: 1260 us
  waiting for transfers between devices  1030 us (81%)
  blocking collectives  133 us (10%)
  matrix products  39.8 us (3%)
  other arithmetic  20 us (2%)
  starting transfers between devices  14.7 us (1%)
  between operations  14 us (1%)
    all_gather x1, waiting for transfers between devices, run_panel(): work_now = lax.all_gather(local, axis_name=('section', 'expert'))  763 us
    all_gather x1, waiting for transfers between devices, shards(): lax.all_gather(tokens, 'section', axis=1, tiled=True)  88.7 us
    psum x1, blocking collectives, shards(): lax.psum((jnp.sum(cot_float * out_first, axis=1), jnp.sum(cot_float * out...  71.3 us
    all_to_all x1, blocking collectives, shards(): lax.all_to_all(sent_cot.reshape(block_shape), 'expert', split_axis=0, con...  61.3 us
    reduce_scatter x1, waiting for transfers between devices, shards(): lax.psum_scatter(forward_part.astype(jnp.bfloat16), 'section', scatter_di...  56.3 us
    all_to_all x1, waiting for transfers between devices, shards(): lax.all_to_all(sent_in.reshape(block_shape), 'expert', split_axis=0, conc...  53.5 us
    reduce_scatter x1, waiting for transfers between devices, shards(): lax.psum_scatter(backward_part.astype(jnp.bfloat16), 'section', scatter_d...  35.8 us
  transfers between devices with their start and end apart: 8, of which 8 were waited for; matrix products, arithmetic and copies ran while one was open for 3% of the time, Pallas kernels for 0%

profile of v1, /device:TPU:1, one launch (start us, length us, event | category | flops | bytes accessed | tf_op | source)
XLA Modules:
  0.0 1260.7 jit_solution(17843219032132230114)
XLA Ops:
  7.2 1.8 copy.35
  9.7 88.7 %all-gather.4.cloned.1.call-done = bf16[192,6144]{0,1:T(8,128)(2,1)} async-done(((bf16[192,192]{0,1:T(8,128)(2,1)}), bf16[192,6144]{0,1:T(8,128)(2,1)}) %all-gather.4.cloned.1.call-update) | async-done | bytes 2359312 | tf_op jit(solution)/shard_map/all_gather | solution.py:43
  98.5 3.4 fusion.39
  101.8 0.7 select_reduce_fusion.1
  102.8 3.6 convolution_convert_fusion.2
  106.4 4.7 all-to-all-start
  111.2 0.7 copy.37
  112.0 53.5 %all-to-all-done = bf16[8,48,6144]{2,1,0:T(8,128)(2,1)} async-done(((bf16[8,48,6144]{2,1,0:T(8,128)(2,1)}), bf16[8,48,6144]{2,1,0:T(8,128)(2,1)}, u32[]{:S(2)}, u32[]{:S(2)}) %all-to-all-start) | async-done | bytes 4718624 | tf_op jit(solution)/shard_map/all_to_all | solution.py:51
  165.6 4.7 fusion.6
  170.3 4.0 convolution_convert_fusion.1
  174.4 21.7 %all-gather.6.cloned.1.call-done = bf16[192,6144]{0,1:T(8,128)(2,1)} async-done(((bf16[192,192]{0,1:T(8,128)(2,1)}), bf16[192,6144]{0,1:T(8,128)(2,1)}) %all-gather.6.cloned.1.call-update) | async-done | bytes 2359312 | tf_op jit(solution)/shard_map/all_gather | solution.py:44
  196.1 3.8 multiply_convert_fusion
  200.0 61.3 %all_to_all.20 = bf16[8,48,6144]{2,1,0:T(8,128)(2,1)S(1)} all-to-all(bf16[8,48,6144]{2,1,0:T(8,128)(2,1)S(1)} %bitcast.62), channel_id=1, replica_groups=mesh['section'=32,'expert'=8] {'expert'}, dimensions={0} | all-to-all | bytes 9437184 | tf_op jit(solution)/shard_map/all_to_all | solution.py:54
  261.2 2.2 copy-done.2
  263.5 1.4 fusion.14
  265.6 4.0 convolution_convert_fusion
  269.6 56.3 %reduce-scatter.3.cloned.1.call-done = bf16[384,192]{0,1:T(8,128)(2,1)} async-done(((bf16[384,6144]{0,1:T(8,128)(2,1)}), bf16[384,192]{0,1:T(8,128)(2,1)}) %reduce-scatter.3.cloned.1.call-update) | async-done | bytes 147472 | tf_op jit(solution)/shard_map/reduce_scatter | solution.py:80
  325.9 1.7 copy.36
  327.6 4.9 all-to-all-start.1
  332.5 5.7 all-to-all-done.1
  338.9 71.3 %all-reduce = (f32[192]{0:T(256)S(1)}, f32[192]{0:T(256)S(1)}) all-reduce(f32[192]{0:T(256)S(1)} %get-tuple-element.26, f32[192]{0:T(256)S(1)} %get-tuple-element.25), channel_id=1, replica_groups=mesh['section'=32,'expert'=8] {'section'}, use_global_device_ids=true, to_apply=%region_6.0 | all-reduce | flops 384 | bytes 3072 | tf_op jit(solution)/shard_map/psum | solution.py:113
  411.4 6.0 fusion.1
  417.4 5.9 fusion
  423.3 35.8 %reduce-scatter.5.cloned.1.call-done = bf16[384,192]{0,1:T(8,128)(2,1)} async-done(((bf16[384,6144]{0,1:T(8,128)(2,1)}), bf16[384,192]{0,1:T(8,128)(2,1)}) %reduce-scatter.5.cloned.1.call-update) | async-done | bytes 147472 | tf_op jit(solution)/shard_map/reduce_scatter | solution.py:83
  459.1 1.7 copy.38
  460.9 4.9 all-to-all-start.3
  465.7 0.7 copy.40
  466.5 1.1 fusion.33
  467.6 3.9 all-to-all-done.3
  471.8 0.9 fusion.18
  472.7 763.1 %all-gather.8.cloned.1.call-done = f32[256,6144,8]{1,2,0:T(8,128)} async-done(((f32[1,6144,8]{1,2,0:T(8,128)}), f32[256,6144,8]{1,2,0:T(8,128)}) %all-gather.8.cloned.1.call-update) | async-done | bytes 50331664 | tf_op jit(solution)/shard_map/all_gather | solution.py:28
  1235.8 18.4 %reduce_sum.59 = f32[6144,8]{0,1:T(8,128)} reduce(f32[256,6144,8]{1,2,0:T(8,128)} %all-gather.8.cloned.1.call-done, f32[]{:T(128)} %constant.9.clone.1), dimensions={0}, to_apply=%region_9.0 | reduce | flops 12533760 | bytes 50528260 | tf_op jit(solution)/shard_map/reduce_sum | solution.py:29
  (49 shorter events, 4.0 us)
Async XLA Ops:
  7.2 163.1 %copy-start = (bf16[1,256,6144]{2,1,0:T(8,128)(2,1)S(1)}, bf16[1,256,6144]{2,1,0:T(8,128)(2,1)}, u32[]{:S(2)}) copy-start(bf16[1,256,6144]{2,1,0:T(8,128)(2,1)} %param.12) | copy-start | bytes 9437188
  7.2 91.3 %all-gather.4.cloned.1.call-start = ((), (), s32[]{:S(2)}) async-start(), calls=%async_computation.6 | async-start | bytes 3244032 | tf_op jit(solution)/shard_map/all_gather | solution.py:43
  98.5 4.3 copy-start.3
  102.8 3.6 copy-start.5
  106.4 4.8 copy-start.11
  106.4 59.2 %all-to-all-start = ((bf16[8,48,6144]{2,1,0:T(8,128)(2,1)}), bf16[8,48,6144]{2,1,0:T(8,128)(2,1)}, u32[]{:S(2)}, u32[]{:S(2)}) async-start(bf16[8,48,6144]{2,1,0:T(8,128)(2,1)} %bitcast.61), calls=%async_computation | async-start | bytes 9437184 | tf_op jit(solution)/shard_map/all_to_all | solution.py:51
  111.2 85.0 %all-gather.6.cloned.1.call-start = ((), (), s32[]{:S(2)}) async-start(), calls=%async_computation.8 | async-start | bytes 3244032 | tf_op jit(solution)/shard_map/all_gather | solution.py:44
  112.0 213.9 %reduce-scatter.3.cloned.1.call-start = ((), (), s32[]{:S(2)}) async-start(), calls=%async_computation.7 | async-start | bytes 4866048 | tf_op jit(solution)/shard_map/reduce_scatter | solution.py:80
  174.4 284.8 %reduce-scatter.5.cloned.1.call-start = ((), (), s32[]{:S(2)}) async-start(), calls=%async_computation.9 | async-start | bytes 4866048 | tf_op jit(solution)/shard_map/reduce_scatter | solution.py:83
  261.2 2.2 copy-start.2
  263.5 2.1 copy-start.4
  264.9 0.7 copy-start.9
  265.6 4.0 copy-start.12
  269.5 69.0 %copy-start.8 = (bf16[192,192]{0,1:T(8,128)(2,1)S(1)}, bf16[192,192]{0,1:T(8,128)(2,1)}, u32[]{:S(2)}) copy-start(bf16[192,192]{0,1:T(8,128)(2,1)} %copy.37) | copy-start | bytes 221188
  269.5 140.6 %copy-start.7 = (bf16[192,192]{1,0:T(8,128)(2,1)S(1)}, bf16[192,192]{1,0:T(8,128)(2,1)}, u32[]{:S(2)}) copy-start(bf16[192,192]{1,0:T(8,128)(2,1)} %param.7) | copy-start | bytes 221188
  327.6 10.6 all-to-all-start.1
  332.5 903.3 %all-gather.8.cloned.1.call-start = ((), (), s32[]{:S(2)}) async-start(), calls=%async_computation.10 | async-start | bytes 50528256 | tf_op jit(solution)/shard_map/all_gather | solution.py:28
  410.7 0.7 copy-start.6
  411.4 6.0 copy-start.10
  460.9 10.7 all-to-all-start.3
  1235.8 18.4 %copy-start.1 = (bf16[1,256,6144]{2,1,0:T(8,128)(2,1)S(1)}, bf16[1,256,6144]{2,1,0:T(8,128)(2,1)}, u32[]{:S(2)}) copy-start(bf16[1,256,6144]{2,1,0:T(8,128)(2,1)} %param.12) | copy-start | bytes 9437188
Sparse Core Ops, SparseCore 0:
  11.3 87.0 all-gather.3
  115.3 80.7 all-gather.5
  200.4 125.4 reduce-scatter.2
  330.0 129.0 reduce-scatter.4
  460.8 774.8 all-gather.7
